TPU v7x, 512 devices: a whole 4x4x16 slice. The times are simulated.
512 devices in a mesh: dp: 32 (over x_lo, z), seq: 4 (over y), mp: 4 (over x_hi, core).
Axes of the slice: x: 4 (x_hi: 2, x_lo: 2; x = x_hi * 2 + x_lo), y: 4, z: 16, core: 2. Of those that a mesh axis runs over, the one named last changes fastest.
Arguments:
- hidden: bfloat16 [32768, 6656], P(('dp', 'seq'), 'mp'), may hold values from -6 to 6
- cotangent: bfloat16 [32768, 17920], P(('dp', 'seq'), 'mp'), may hold values from -6 to 6
- frozen_down: bfloat16 [6656, 4], P('mp'), may hold values from -0.078125 to 0.078125
- adapter: float32 [4, 4, 4480], P('mp', None, ('dp', 'seq')), may hold values from -6 to 6
- prior: float32 [48], replicated, may hold values from 0.2 to 5
- domain_of: int32 [64], P('dp'), may hold values from 0 to 47
Outputs:
- new_adapter: float32 [4, 4, 4480], P('mp', None, ('dp', 'seq'))
- log_weights: float32 [48], replicated
All inputs are finite; a program needn't handle non-finite values.
Results may differ from a plain program's by a relative error of at most 0.014.
Values may be sent and summed in bfloat16 or wider, within the bound.
A program may use at most 64 MiB of HBM per device.

v0:
```python
import jax
import jax.numpy as jnp
from jax import lax
from jax.sharding import PartitionSpec as P

FF = 17920
NDOM = 48
RANK = 4
step_rate = 1.0
learn_rate = 0.5


def expand_weights(weights):
    return (weights[:, None, None] * jnp.eye(RANK, dtype=jnp.float32)[None, :, :]).reshape(
        NDOM * RANK, RANK
    )


def domain_scores(terms, mixture):
    return jnp.sum(terms.reshape(terms.shape[0], NDOM, RANK) * mixture[:, None, :], axis=(0, 2))


def reweight(weights, scores, sumsq):
    meansq = sumsq / (RANK * FF) + 1e-06
    ratio = scores / (RANK * FF * meansq)
    raised = weights * jnp.exp(step_rate * ratio)
    log_new = jnp.log(weights) + step_rate * ratio - jnp.log(jnp.sum(raised))
    return (log_new, meansq)


def body(hidden, cotangent, frozen_down, adapter, prior, domain_of):
    rows = hidden.shape[0]
    piece = rows // domain_of.shape[0]
    partial_down = jnp.dot(hidden, frozen_down, preferred_element_type=jnp.float32)
    down = lax.psum(partial_down.astype(jnp.bfloat16), "mp")
    domain_tok = jnp.repeat(domain_of, piece, total_repeat_length=rows)
    onehot = (domain_tok[:, None] == jnp.arange(NDOM, dtype=jnp.int32)[None, :]).astype(
        jnp.bfloat16
    )
    spread = (onehot[:, :, None] * down[:, None, :]).reshape(rows, NDOM * RANK)
    weights = prior / jnp.sum(prior)
    highest = lax.Precision.HIGHEST
    shard = lax.psum_scatter(
        lax.dot_general(
            cotangent, spread, (((0,), (0,)), ((), ())), preferred_element_type=jnp.float32
        ),
        ("dp", "seq"),
        scatter_dimension=0,
        tiled=True,
    )
    mixture = jnp.dot(shard, expand_weights(weights), precision=highest)
    scores, sumsq = lax.psum(
        (domain_scores(shard, mixture), jnp.sum(mixture * mixture)), ("dp", "seq", "mp")
    )
    log_new, meansq = reweight(weights, scores, sumsq)
    update = jnp.dot(shard, expand_weights(jnp.exp(log_new)), precision=highest)
    new_adapter = adapter - learn_rate * update.T[None, :, :] / jnp.sqrt(meansq)
    return (new_adapter, log_new)


def solution(mesh):
    return jax.shard_map(
        body,
        mesh=mesh,
        in_specs=(
            P(("dp", "seq"), "mp"),
            P(("dp", "seq"), "mp"),
            P("mp", None),
            P("mp", None, ("dp", "seq")),
            P(),
            P("dp"),
        ),
        out_specs=(P("mp", None, ("dp", "seq")), P()),
        check_vma=False,
    )
```

profile of v0, /device:TPU:1, one launch (start us, length us, event | category | flops | bytes accessed | tf_op | source)
XLA Modules:
  0.0 1317.5 jit_solution(4457269442039612143)
XLA Ops:
  7.2 0.0 all-reduce.4.cloned.1.call-start
  7.2 1.4 fusion.17
  8.7 1.3 compare_select_fusion.1
  10.0 1.4 convolution_convert_fusion
  11.4 13.4 %psum.21 = bf16[256,4]{0,1:T(4,128)(2,1)S(1)} all-reduce(bf16[256,4]{0,1:T(4,128)(2,1)S(1)} %convolution_convert_fusion), channel_id=1, replica_groups=mesh['dp'=32,'seq'=4,'mp'=4] {'mp'}, use_global_device_ids=true, to_apply=%region_1.2 | all-reduce | flops 1024 | bytes 4096 | tf_op jit(solution)/shard_map/psum | solution.py:35
  24.9 0.1 broadcast_multiply_fusion
  25.0 2.4 convolution_bitcast_fusion
  27.4 0.6 copy-done.2
  28.0 0.6 reduce_sum.43
  28.6 0.6 broadcast_divide_fusion.1
  29.3 0.1 mul.88
  29.4 0.1 mul.89
  29.5 1.3 dynamic-slice.6
  31.4 1092.8 %all-reduce.4.cloned.1.call-done = f32[4480,192]{0,1:T(8,128)} async-done(((f32[4480,192]{0,1:T(8,128)}), f32[4480,192]{0,1:T(8,128)}) %all-reduce.4.cloned.1.call-update) | async-done | bytes 3440656
  1124.3 1.9 multiply_reduce_fusion.1
  1126.2 1.1 multiply_reduce_fusion
  1127.3 0.1 reduce_sum.45
  1127.5 0.1 reduce_sum.46
  1127.6 177.2 %all-reduce.1 = (f32[48]{0:T(128)S(1)}, f32[]{:T(128)}) all-reduce(f32[48]{0:T(128)S(1)} %reduce_sum.46, f32[]{:T(128)} %get-tuple-element.22), channel_id=1, replica_groups=mesh['dp'=32,'seq'=4,'mp'=4] {'dp','seq','mp'}, use_global_device_ids=true, to_apply=%region_5.6 | all-reduce | flops 49 | bytes 392 | tf_op jit(solution)/shard_map/psum | solution.py:52
  1305.4 1.3 multiply_reduce_fusion.2
  1307.4 1.2 fusion.16
  1308.6 0.1 mul.100
  1308.6 0.1 mul.101
  1308.8 1.9 fusion.2
  (14 shorter events, 0.1 us)
Async XLA Ops:
  7.2 17.8 %copy-start = (bf16[256,4480]{1,0:T(8,128)(2,1)S(1)}, bf16[256,4480]{1,0:T(8,128)(2,1)}, u32[]{:S(2)}) copy-start(bf16[256,4480]{1,0:T(8,128)(2,1)} %param.9) | copy-start | bytes 6881284
  7.2 1117.1 %all-reduce.4.cloned.1.call-start = ((), (), s32[]{:S(2)}) async-start(), calls=%async_computation | async-start | bytes 6881280
  27.4 0.7 copy-start.2
  27.4 1281.4 %copy-start.1 = (f32[1,4,35]{2,1,0:T(4,128)S(1)}, f32[1,4,35]{2,1,0:T(4,128)}, u32[]{:S(2)}) copy-start(f32[1,4,35]{2,1,0:T(4,128)} %param.11) | copy-start | bytes 1684
Sparse Core Ops, SparseCore 0:
  27.5 1096.6 all-reduce.3
where the time goes:
time: 1320 us
  waiting for transfers between devices  1090 us (83%)
  blocking collectives  191 us (14%)
  between operations  16.2 us (1%)
    unnamed x2, waiting for transfers between devices  1090 us
    psum x1, blocking collectives, body(): lax.psum((domain_scores(shard, mixture), jnp.sum(mixture * mixture)), ('d...  177 us
  transfers between devices with their start and end apart: 1, of which 1 were waited for; matrix products, arithmetic and copies ran while one was open for 0% of the time, Pallas kernels for 0%

commit v1 on v0

--- a/solution.py
+++ b/solution.py
@@ -49,8 +49,13 @@
         tiled=True,
     )
     mixture = jnp.dot(shard, expand_weights(weights), precision=highest)
-    scores, sumsq = lax.psum(
-        (domain_scores(shard, mixture), jnp.sum(mixture * mixture)), ("dp", "seq", "mp")
+
+    def _note_cubes(block_here, dev_axis, along_axis):
+        local_part = lax.psum(block_here, dev_axis)
+        return lax.psum(local_part, along_axis)
+
+    scores, sumsq = _note_cubes(
+        (domain_scores(shard, mixture), jnp.sum(mixture * mixture)), "dp", ("seq", "mp")
     )
     log_new, meansq = reweight(weights, scores, sumsq)
     update = jnp.dot(shard, expand_weights(jnp.exp(log_new)), precision=highest)

time: 1320 us -> 1310 us (level)
    psum x1 -> x2, blocking collectives: 177 us -> 170 us  [the longest x1 121 us: _note_cubes(): return lax.psum(local_part, along_axis)]
where the time goes in v1:
time: 1310 us
  waiting for transfers between devices  1090 us (83%)
  blocking collectives  184 us (14%)
  between operations  16.2 us (1%)
    unnamed x2, waiting for transfers between devices  1090 us
    psum x1, blocking collectives, _note_cubes(): return lax.psum(local_part, along_axis)  121 us
    psum x1, blocking collectives, _note_cubes(): local_part = lax.psum(block_here, dev_axis)  49.4 us
  transfers between devices with their start and end apart: 1, of which 1 were waited for; matrix products, arithmetic and copies ran while one was open for 0% of the time, Pallas kernels for 0%

profile of v1, /device:TPU:1, one launch (start us, length us, event | category | flops | bytes accessed | tf_op | source)
XLA Modules:
  0.0 1310.6 jit_solution(15635422688329075307)
XLA Ops:
  7.2 1.4 fusion.17
  8.7 1.3 compare_select_fusion.1
  10.0 1.4 convolution_convert_fusion
  11.4 13.4 %psum.35 = bf16[256,4]{0,1:T(4,128)(2,1)S(1)} all-reduce(bf16[256,4]{0,1:T(4,128)(2,1)S(1)} %convolution_convert_fusion), channel_id=1, replica_groups=mesh['dp'=32,'seq'=4,'mp'=4] {'mp'}, use_global_device_ids=true, to_apply=%region_1.2 | all-reduce | flops 1024 | bytes 4096 | tf_op jit(solution)/shard_map/psum | solution.py:35
  24.9 0.1 broadcast_multiply_fusion
  25.0 2.4 convolution_bitcast_fusion
  27.4 0.6 copy-done.2
  28.0 0.6 reduce_sum.43
  28.6 0.6 broadcast_divide_fusion.1
  29.3 0.1 mul.88
  29.4 0.1 mul.89
  29.5 1.3 dynamic-slice.6
  31.4 1092.8 %all-reduce.5.cloned.1.call-done = f32[4480,192]{0,1:T(8,128)} async-done(((f32[4480,192]{0,1:T(8,128)}), f32[4480,192]{0,1:T(8,128)}) %all-reduce.5.cloned.1.call-update) | async-done | bytes 3440656
  1124.3 1.9 multiply_reduce_fusion.1
  1126.2 1.1 multiply_reduce_fusion
  1127.3 0.1 reduce_sum.45
  1127.5 0.1 reduce_sum.46
  1127.6 49.4 %all-reduce.1 = (f32[48]{0:T(128)S(1)}, f32[]{:T(128)}) all-reduce(f32[48]{0:T(128)S(1)} %reduce_sum.46, f32[]{:T(128)} %get-tuple-element.24), channel_id=1, replica_groups=mesh['dp'=32,'seq'=4,'mp'=4] {'dp'}, use_global_device_ids=true, to_apply=%region_5.6 | all-reduce | flops 49 | bytes 392 | tf_op jit(solution)/shard_map/psum | solution.py:54
  1177.0 120.9 %all-reduce.2 = (f32[48]{0:T(128)S(1)}, f32[]{:T(128)}) all-reduce(f32[48]{0:T(128)S(1)} %get-tuple-element.14, f32[]{:T(128)} %get-tuple-element.15), channel_id=1, replica_groups=mesh['dp'=32,'seq'=4,'mp'=4] {'seq','mp'}, use_global_device_ids=true, to_apply=%region_6.7 | all-reduce | flops 49 | bytes 392 | tf_op jit(solution)/shard_map/psum | solution.py:55
  1298.6 1.3 multiply_reduce_fusion.2
  1300.5 1.2 fusion.16
  1301.7 0.1 mul.100
  1301.8 0.1 mul.101
  1301.9 1.9 fusion.2
  (15 shorter events, 0.2 us)
Async XLA Ops:
  7.2 17.8 %copy-start = (bf16[256,4480]{1,0:T(8,128)(2,1)S(1)}, bf16[256,4480]{1,0:T(8,128)(2,1)}, u32[]{:S(2)}) copy-start(bf16[256,4480]{1,0:T(8,128)(2,1)} %param.9) | copy-start | bytes 6881284
  7.2 1117.1 %all-reduce.5.cloned.1.call-start = ((), (), s32[]{:S(2)}) async-start(), calls=%async_computation | async-start | bytes 6881280
  27.4 0.7 copy-start.2
  27.4 1274.5 %copy-start.1 = (f32[1,4,35]{2,1,0:T(4,128)S(1)}, f32[1,4,35]{2,1,0:T(4,128)}, u32[]{:S(2)}) copy-start(f32[1,4,35]{2,1,0:T(4,128)} %param.11) | copy-start | bytes 1684
Sparse Core Ops, SparseCore 0:
  27.5 1096.6 all-reduce.4
